TPU v7x, 32 devices: a whole 2x2x4 slice. The times are simulated.
32 devices in a mesh: dp: 8 (over z, y), tp: 4 (over x, core).
Axes of the slice: x: 2, y: 2, z: 4, core: 2. Of those that a mesh axis runs over, the one named last changes fastest.
Arguments:
- tokens: bfloat16 [32, 1024, 768], P(('dp', 'tp')), may hold values from -11 to 11
- clip_lengths: int32 [32, 4], P(('dp', 'tp')), may hold values from 1 to 384, as said below
- out_grad: bfloat16 [32, 1024, 768], P(('dp', 'tp')), may hold values from -6 to 6
- w_query: bfloat16 [768, 768], P(('dp', 'tp')), may hold values from -0.21875 to 0.21875
- w_key: bfloat16 [768, 768], P(('dp', 'tp')), may hold values from -0.21875 to 0.21875
- w_value: bfloat16 [768, 768], P(('dp', 'tp')), may hold values from -0.21875 to 0.21875
- w_output: bfloat16 [768, 768], P(('dp', 'tp')), may hold values from -2.5 to 2.5
- gain_attention: bfloat16 [768], P(('dp', 'tp')), may hold values from 0.099609375 to 1.8984375
- gain_feed: bfloat16 [768], P(('dp', 'tp')), may hold values from 0.099609375 to 1.8984375
- w_expand: bfloat16 [768, 3072], P('dp', 'tp'), may hold values from -0.21875 to 0.21875
- w_reduce: bfloat16 [3072, 768], P('tp', 'dp'), may hold values from -0.4375 to 0.4375
Outputs:
- block_out: bfloat16 [32, 1024, 768], P(('dp', 'tp'))
- grad_tokens: float32 [32, 1024, 768], P(('dp', 'tp'))
- grad_w_query: float32 [768, 768], P(('dp', 'tp'))
- grad_w_key: float32 [768, 768], P(('dp', 'tp'))
- grad_w_value: float32 [768, 768], P(('dp', 'tp'))
- grad_w_output: float32 [768, 768], P(('dp', 'tp'))
- grad_gain_attention: float32 [768], P(('dp', 'tp'))
- grad_gain_feed: float32 [768], P(('dp', 'tp'))
- grad_w_expand: float32 [768, 3072], P('dp', 'tp')
- grad_w_reduce: float32 [3072, 768], P('tp', 'dp')
- root_mean_squares: float32 [3], replicated
Inputs may be any that keep to these rules, and one draw needn't show every extreme that they name: Each row of clip_lengths gives the lengths of its 3 clips in order, each at most 384 with one of exactly 384 in every row, then the number of padding slots at the row's end, 1 to 256; a row's entries sum to 1024.
All inputs are finite; a program needn't handle non-finite values.
Results may differ from a plain program's by a relative error of at most 0.015.
Values may be sent and summed in bfloat16 or wider, within the bound.
A program may use at most 192 MiB of HBM per device.

v0:
```python
from functools import partial
import jax
import jax.numpy as jnp
from jax import lax
from jax.sharding import PartitionSpec as P

HEADS = 12
HEAD_DIM = 64
SLOTS = 4


def segment_numbers(lengths, pack_len):
    clip_ends = jnp.cumsum(lengths[:, :-1], axis=-1, dtype=jnp.int32)
    position = jnp.arange(pack_len, dtype=jnp.int32)
    return jnp.sum(
        (position[None, :, None] >= clip_ends[:, None, :]).astype(jnp.int32),
        axis=-1,
        dtype=jnp.int32,
    )


def normalize(array_in):
    average = jnp.mean(array_in, axis=-1, keepdims=True)
    centred = array_in - average
    spread = jnp.mean(centred * centred, axis=-1, keepdims=True)
    inv_scale = lax.rsqrt(spread + 1e-06)
    return (centred * inv_scale, inv_scale)


def norm_back(grad_normed, unit_value, inv_scale, gain_vec):
    scaled = grad_normed * gain_vec
    inner_sum = (
        scaled
        - jnp.mean(scaled, axis=-1, keepdims=True)
        - unit_value * jnp.mean(scaled * unit_value, axis=-1, keepdims=True)
    )
    return (inv_scale * inner_sum, jnp.sum(grad_normed * unit_value, axis=0))


def dot_plain(left_side, right_side):
    return jnp.dot(left_side, right_side, preferred_element_type=jnp.float32)


def dot_first(left_side, right_side):
    return lax.dot_general(
        left_side, right_side, (((0,), (0,)), ((), ())), preferred_element_type=jnp.float32
    )


def dot_last(left_side, right_side):
    return lax.dot_general(
        left_side, right_side, (((1,), (1,)), ((), ())), preferred_element_type=jnp.float32
    )


def split_heads(array_in, rows_dev, pack_len):
    return (
        array_in.reshape(rows_dev, pack_len, HEADS, HEAD_DIM)
        .transpose(0, 2, 1, 3)
        .reshape(rows_dev * HEADS, pack_len, HEAD_DIM)
    )


def merge_heads(array_in, rows_dev, pack_len):
    return (
        array_in.reshape(rows_dev, HEADS, pack_len, HEAD_DIM)
        .transpose(0, 2, 1, 3)
        .reshape(rows_dev * pack_len, HEADS * HEAD_DIM)
    )


def head_scores(query_head, key_head, segments):
    same_clip = segments[:, None] == segments[None, :]
    scores = dot_last(query_head, key_head) * 0.125
    return jnp.where(same_clip, scores, -1e30)


def head_forward(block_item):
    query_head, key_head, value_head, segments = block_item
    scores = head_scores(query_head, key_head, segments)
    row_max = jnp.max(scores, axis=-1, keepdims=True)
    exponent = jnp.exp(scores - row_max)
    row_sum = jnp.sum(exponent, axis=-1, keepdims=True)
    weights = (exponent / row_sum).astype(jnp.bfloat16)
    return (dot_plain(weights, value_head).astype(jnp.bfloat16), row_max, row_sum)


def head_backward(block_item):
    query_head, key_head, value_head, segments, row_max, row_sum, grad_head = block_item
    scores = head_scores(query_head, key_head, segments)
    probabilities = jnp.exp(scores - row_max) / row_sum
    grad_probs = dot_last(grad_head, value_head)
    grad_value = dot_first(probabilities.astype(jnp.bfloat16), grad_head)
    inner_sum = jnp.sum(probabilities * grad_probs, axis=-1, keepdims=True)
    grad_scores = (probabilities * (grad_probs - inner_sum)).astype(jnp.bfloat16)
    grad_query = (dot_plain(grad_scores, key_head) * 0.125).astype(jnp.bfloat16)
    grad_key = (dot_first(grad_scores, query_head) * 0.125).astype(jnp.bfloat16)
    return (grad_query, grad_key, grad_value.astype(jnp.bfloat16))


def on_device(
    tokens,
    clip_lengths,
    out_grad,
    w_query,
    w_key,
    w_value,
    w_output,
    gain_attention,
    gain_feed,
    w_expand,
    w_reduce,
):
    rows_dev, pack_len, width = tokens.shape
    token_count = rows_dev * pack_len
    segments = segment_numbers(clip_lengths, pack_len)
    valid_rows = (segments < SLOTS - 1).astype(jnp.float32).reshape(-1)
    valid_column = valid_rows[:, None]
    inputs = tokens.reshape(token_count, width).astype(jnp.float32)
    query_full, key_full, value_full, output_full, gain_one, gain_two = (
        lax.all_gather(w_query, ("dp", "tp"), axis=0, tiled=True),
        lax.all_gather(w_key, ("dp", "tp"), axis=0, tiled=True),
        lax.all_gather(w_value, ("dp", "tp"), axis=0, tiled=True),
        lax.all_gather(w_output, ("dp", "tp"), axis=0, tiled=True),
        lax.all_gather(gain_attention, ("dp", "tp"), axis=0, tiled=True),
        lax.all_gather(gain_feed, ("dp", "tp"), axis=0, tiled=True),
    )
    expand_full, reduce_full = (
        lax.all_gather(w_expand, "dp", axis=0, tiled=True),
        lax.all_gather(w_reduce, "dp", axis=1, tiled=True),
    )
    gain_one = gain_one.astype(jnp.float32)
    gain_two = gain_two.astype(jnp.float32)
    unit_one, scale_one = normalize(inputs)
    normed = (unit_one * gain_one).astype(jnp.bfloat16)
    query_rows = dot_plain(normed, query_full).astype(jnp.bfloat16)
    key_rows = dot_plain(normed, key_full).astype(jnp.bfloat16)
    value_rows = dot_plain(normed, value_full).astype(jnp.bfloat16)
    head_segments = jnp.repeat(segments, HEADS, axis=0)
    query_heads = split_heads(query_rows, rows_dev, pack_len)
    key_heads = split_heads(key_rows, rows_dev, pack_len)
    value_heads = split_heads(value_rows, rows_dev, pack_len)
    mixed_heads, row_maxima, row_sums = lax.map(
        head_forward, (query_heads, key_heads, value_heads, head_segments)
    )
    mixed_rows = merge_heads(mixed_heads, rows_dev, pack_len)
    branch = dot_plain(mixed_rows, output_full)
    middle = inputs + branch
    unit_two, scale_two = normalize(middle)
    normed_feed = (unit_two * gain_two).astype(jnp.bfloat16)
    normed_rows = lax.all_gather(normed_feed, "tp", axis=0, tiled=True)
    hidden = dot_plain(normed_rows, expand_full)
    gelu_value, gelu_pull = jax.vjp(partial(jax.nn.gelu, approximate=False), hidden)
    active = gelu_value.astype(jnp.bfloat16)
    feed_out = lax.psum_scatter(
        dot_plain(
            lax.slice_in_dim(active, 0, token_count * lax.axis_size("tp"), axis=0), reduce_full
        ),
        "tp",
        scatter_dimension=0,
        tiled=True,
    )
    result = (middle + feed_out).astype(jnp.bfloat16).reshape(rows_dev, pack_len, width)
    totals_all = lax.psum(
        (
            jnp.sum(inputs * inputs * valid_column),
            jnp.sum(branch * branch * valid_column),
            jnp.sum(feed_out * feed_out * valid_column),
            jnp.sum(valid_rows),
        ),
        ("dp", "tp"),
    )
    rms_stats = jnp.sqrt(jnp.stack(totals_all[:3]) / (totals_all[3] * width))
    grad_result = out_grad.reshape(token_count, width).astype(jnp.float32) * valid_column
    grad_feed = grad_result.astype(jnp.bfloat16)
    grad_rows = lax.all_gather(grad_feed, "tp", axis=0, tiled=True)
    grad_reduce = dot_first(active, grad_rows)
    grad_active = dot_last(grad_rows, reduce_full)
    grad_hidden = gelu_pull(grad_active)[0].astype(jnp.bfloat16)
    grad_expand = dot_first(normed_rows, grad_hidden)
    grad_normed_feed = lax.psum_scatter(
        dot_last(grad_hidden, expand_full), "tp", scatter_dimension=0, tiled=True
    )
    grad_norm_two, grad_gain_two = norm_back(grad_normed_feed, unit_two, scale_two, gain_two)
    grad_middle = grad_result + grad_norm_two
    grad_branch = grad_middle.astype(jnp.bfloat16)
    grad_output_w = dot_first(mixed_rows, grad_branch)
    grad_mixed = dot_last(grad_branch, output_full).astype(jnp.bfloat16)
    grad_heads = split_heads(grad_mixed, rows_dev, pack_len)
    grad_query_heads, grad_key_heads, grad_value_heads = lax.map(
        head_backward,
        (query_heads, key_heads, value_heads, head_segments, row_maxima, row_sums, grad_heads),
    )
    grad_query = merge_heads(grad_query_heads, rows_dev, pack_len)
    grad_key = merge_heads(grad_key_heads, rows_dev, pack_len)
    grad_value = merge_heads(grad_value_heads, rows_dev, pack_len)
    grad_query_w = dot_first(normed, grad_query)
    grad_key_w = dot_first(normed, grad_key)
    grad_value_w = dot_first(normed, grad_value)
    grad_normed = (
        dot_last(grad_query, query_full)
        + dot_last(grad_key, key_full)
        + dot_last(grad_value, value_full)
    )
    grad_norm_one, grad_gain_one = norm_back(grad_normed, unit_one, scale_one, gain_one)
    grad_inputs = (grad_middle + grad_norm_one).reshape(rows_dev, pack_len, width)
    shard_expand, shard_reduce = (
        lax.psum_scatter(grad_expand, "dp", scatter_dimension=0, tiled=True),
        lax.psum_scatter(grad_reduce, "dp", scatter_dimension=1, tiled=True),
    )
    shard_query, shard_key, shard_value, shard_output, shard_gain_one, shard_gain_two = (
        lax.psum_scatter(grad_query_w, ("dp", "tp"), scatter_dimension=0, tiled=True),
        lax.psum_scatter(grad_key_w, ("dp", "tp"), scatter_dimension=0, tiled=True),
        lax.psum_scatter(grad_value_w, ("dp", "tp"), scatter_dimension=0, tiled=True),
        lax.psum_scatter(grad_output_w, ("dp", "tp"), scatter_dimension=0, tiled=True),
        lax.psum_scatter(grad_gain_one, ("dp", "tp"), scatter_dimension=0, tiled=True),
        lax.psum_scatter(grad_gain_two, ("dp", "tp"), scatter_dimension=0, tiled=True),
    )
    return (
        result,
        grad_inputs,
        shard_query,
        shard_key,
        shard_value,
        shard_output,
        shard_gain_one,
        shard_gain_two,
        shard_expand,
        shard_reduce,
        rms_stats,
    )


def solution(mesh):
    in_specs = (
        P(("dp", "tp"), None, None),
        P(("dp", "tp"), None),
        P(("dp", "tp"), None, None),
        P(("dp", "tp"), None),
        P(("dp", "tp"), None),
        P(("dp", "tp"), None),
        P(("dp", "tp"), None),
        P(("dp", "tp")),
        P(("dp", "tp")),
        P("dp", "tp"),
        P("tp", "dp"),
    )
    out_specs = (
        P(("dp", "tp"), None, None),
        P(("dp", "tp"), None, None),
        P(("dp", "tp"), None),
        P(("dp", "tp"), None),
        P(("dp", "tp"), None),
        P(("dp", "tp"), None),
        P(("dp", "tp")),
        P(("dp", "tp")),
        P("dp", "tp"),
        P("tp", "dp"),
        P(),
    )
    return jax.shard_map(
        on_device, mesh=mesh, in_specs=in_specs, out_specs=out_specs, check_vma=False
    )
```

profile of v0, /device:TPU:0, one launch (start us, length us, event | category | flops | bytes accessed | tf_op | source)
XLA Modules:
  0.0 1258.4 jit_solution(7682637012286789652)
XLA Ops:
  13.2 42.1 %all-reduce.5 = (bf16[768]{0:T(1024)(128)(2,1)S(1)}, bf16[768]{0:T(1024)(128)(2,1)S(1)}) all-reduce(bf16[768]{0:T(1024)(128)(2,1)S(1)} %dynamic-update-slice, bf16[768]{0:T(1024)(128)(2,1)S(1)} %dynamic-update-slice.1), channel_id=1, replica_groups=mesh['dp'=8,'tp'=4] {'dp','tp'}, use_global_device_ids=true, to_apply=%add | all-reduce | flops 1536 | bytes 6144
  56.0 11.7 all-gather.9.cloned.1.call-done
  73.3 50.4 %all-gather.11.cloned.1.call-done = bf16[768,768]{1,0:T(8,128)(2,1)} async-done(((bf16[24,768]{1,0:T(8,128)(2,1)}), bf16[768,768]{1,0:T(8,128)(2,1)}) %all-gather.11.cloned.1.call-update) | async-done | bytes 1179664 | tf_op jit(solution)/shard_map/all_gather | solution.py:122
  129.2 50.3 %all-gather.13.cloned.1.call-done = bf16[768,768]{1,0:T(8,128)(2,1)} async-done(((bf16[24,768]{1,0:T(8,128)(2,1)}), bf16[768,768]{1,0:T(8,128)(2,1)}) %all-gather.13.cloned.1.call-update) | async-done | bytes 1179664 | tf_op jit(solution)/shard_map/all_gather | solution.py:123
  185.4 68.7 %while.28 = (s32[]{:T(128)}, bf16[12,1024,64]{1,2,0:T(8,128)(2,1)S(1)}, f32[12,1024,1]{1,2,0:T(1,128)}, f32[12,1024,1]{1,2,0:T(1,128)}, s32[12,1024]{1,0:T(8,128...) while((s32[]{:T(128)}, ...), condition=%wide.region_7.8_spmd, body=%wide.region_4.7_spmd.sunk | while | flops 284227584 | bytes 13568109 | solution.py:143
  265.7 11.7 all-gather.19.cloned.1.call-done
  277.4 47.2 %all-gather.17.cloned.1.call-done = bf16[4096,768]{0,1:T(8,128)(2,1)} async-done(((bf16[1024,768]{0,1:T(8,128)(2,1)}), bf16[4096,768]{0,1:T(8,128)(2,1)}) %all-gather.17.cloned.1.call-update) | async-done | bytes 6291472 | tf_op jit(solution)/shard_map/all_gather | solution.py:151
  324.5 10.2 fusion.104
  334.7 33.1 %all-gather.21.cloned.1.call-done = bf16[768,768]{0,1:T(8,128)(2,1)} async-done(((bf16[768,96]{0,1:T(8,128)(2,1)}), bf16[768,768]{0,1:T(8,128)(2,1)}) %all-gather.21.cloned.1.call-update) | async-done | bytes 1179664 | tf_op jit(solution)/shard_map/all_gather | solution.py:130
  367.8 46.7 %all-gather.23.cloned.1.call-done = bf16[4096,768]{0,1:T(8,128)(2,1)} async-done(((bf16[1024,768]{0,1:T(8,128)(2,1)}), bf16[4096,768]{0,1:T(8,128)(2,1)}) %all-gather.23.cloned.1.call-update) | async-done | bytes 6291472 | tf_op jit(solution)/shard_map/all_gather | solution.py:176
  414.6 36.4 %add_convert_fusion = (bf16[4096,768]{1,0:T(8,128)(2,1)S(1)}, f32[4096,768]{1,0:T(8,128)}) fusion(f32[4096,768]{1,0:T(8,128)} %fusion.104, bf16[4096,768]{0,1:T(8,128)(2,1)} %all-gather.23.cloned.1.call-done, bf16[768,768]{0,1:T(8,128)(2,1)} %all-gather.21.cloned.1.call-done), kind=kOutput, calls=%fused_computation.64 | convolution fusion | flops 5058330624 | bytes 38928384 | tf_op jit(solution)/shard_map/dot_general | solution.py:51
  453.5 8.0 fusion.106
  461.6 11.3 multiply_convert_fusion.1
  476.6 7.9 fusion.105
  484.6 10.4 fusion.107
  495.1 10.1 fusion.110
  505.3 55.4 %reduce-scatter.11.cloned.1.call-done = f32[1024,768]{0,1:T(8,128)} async-done(((f32[4096,768]{0,1:T(8,128)}), f32[1024,768]{0,1:T(8,128)}) %reduce-scatter.11.cloned.1.call-update) | async-done | bytes 3145744 | tf_op jit(solution)/shard_map/reduce_scatter | solution.py:181
  563.6 98.6 %reduce-scatter.9.cloned.1.call-done = f32[1024,768]{0,1:T(8,128)} async-done(((f32[4096,768]{0,1:T(8,128)}), f32[1024,768]{0,1:T(8,128)}) %reduce-scatter.9.cloned.1.call-update) | async-done | bytes 3145744 | tf_op jit(solution)/shard_map/reduce_scatter | solution.py:155
  676.3 160.4 %while.29 = (s32[]{:T(128)}, bf16[12,1024,64]{1,2,0:T(8,128)(2,1)S(1)}, bf16[12,1024,64]{1,2,0:T(8,128)(2,1)}, bf16[12,1024,64]{1,2,0:T(8,128)(2,1)}, s32[12,102...) while((s32[]{:T(128)}, ...), condition=%wide.region_16.17_spmd, body=%wide.region_14.16_spmd.sunk | while | flops 682949632 | bytes 33739908 | solution.py:190
  870.8 39.8 %all-reduce.4 = (f32[768]{0:T(1024)S(1)}, f32[768]{0:T(1024)S(1)}, f32[1]{0:T(128)}, f32[1]{0:T(128)}, f32[1]{0:T(128)}, /*index=5*/f32[]{:T(128)}) all-reduce(f32[768]{0:T(1024)S(1)} %get-tuple-element.155, f32[768]{0:T(1024)S(1)} %get-tuple-element.153, f32[1]{0:T(128)} %bitcast.60, ...), channel_id=8, replica_groups=mesh['dp'=8,'tp'=4] {'dp','tp'}, use_global_device_ids=true, to_apply=%region_24.25.clone | all-reduce | flops 1540 | bytes 12320
  914.8 23.9 %reduce-scatter.13.cloned.1.call-done = f32[24,768]{1,0:T(8,128)} async-done(((f32[768,768]{1,0:T(8,128)}), f32[24,768]{1,0:T(8,128)}) %reduce-scatter.13.cloned.1.call-update) | async-done | bytes 73744 | tf_op jit(solution)/shard_map/reduce_scatter | solution.py:212
  938.7 104.6 %reduce-scatter.15.cloned.1.call-done = f32[24,768]{1,0:T(8,128)} async-done(((f32[768,768]{1,0:T(8,128)}), f32[24,768]{1,0:T(8,128)}) %reduce-scatter.15.cloned.1.call-update) | async-done | bytes 73744 | tf_op jit(solution)/shard_map/reduce_scatter | solution.py:213
  1043.3 103.7 %reduce-scatter.17.cloned.1.call-done = f32[24,768]{1,0:T(8,128)} async-done(((f32[768,768]{1,0:T(8,128)}), f32[24,768]{1,0:T(8,128)}) %reduce-scatter.17.cloned.1.call-update) | async-done | bytes 73744 | tf_op jit(solution)/shard_map/reduce_scatter | solution.py:214
  1147.0 104.7 %reduce-scatter.19.cloned.1.call-done = f32[24,768]{1,0:T(8,128)} async-done(((f32[768,768]{1,0:T(8,128)}), f32[24,768]{1,0:T(8,128)}) %reduce-scatter.19.cloned.1.call-update) | async-done | bytes 73744 | tf_op jit(solution)/shard_map/reduce_scatter | solution.py:215
  (328 shorter events, 324.4 us)
Async XLA Ops:
  7.2 60.6 %all-gather.9.cloned.1.call-start = ((), (), s32[]{:S(2)}) async-start(), calls=%async_computation.8 | async-start | bytes 1216512 | tf_op jit(solution)/shard_map/all_gather | solution.py:121
  7.9 115.7 %all-gather.11.cloned.1.call-start = ((), (), s32[]{:S(2)}) async-start(), calls=%async_computation.9 | async-start | bytes 1216512 | tf_op jit(solution)/shard_map/all_gather | solution.py:122
  8.7 170.9 %all-gather.13.cloned.1.call-start = ((), (), s32[]{:S(2)}) async-start(), calls=%async_computation.10 | async-start | bytes 1216512 | tf_op jit(solution)/shard_map/all_gather | solution.py:123
  9.4 244.7 %all-gather.15.cloned.1.call-start = ((), (), s32[]{:S(2)}) async-start(), calls=%async_computation.11 | async-start | bytes 1216512 | tf_op jit(solution)/shard_map/all_gather | solution.py:124
  10.0 267.4 %all-gather.19.cloned.1.call-start = ((), (), s32[]{:S(2)}) async-start(), calls=%async_computation.13 | async-start | bytes 1327104 | tf_op jit(solution)/shard_map/all_gather | solution.py:129
  10.6 314.0 %all-gather.17.cloned.1.call-start = ((), (), s32[]{:S(2)}) async-start(), calls=%async_computation.12 | async-start | bytes 7864320 | tf_op jit(solution)/shard_map/all_gather | solution.py:151
  12.4 241.8 %copy-start.2 = (bf16[1,1024,768]{1,2,0:T(8,128)(2,1)}, bf16[1,1024,768]{1,2,0:T(8,128)(2,1)S(1)}, u32[]{:S(2)}) copy-start(bf16[1,1024,768]{1,2,0:T(8,128)(2,1)S(1)} %copy.42) | copy-start | bytes 4718596
  12.7 251.3 %copy-start.19 = (s32[1024]{0:T(1024)}, s32[1024]{0:T(1024)S(1)}, u32[]{:S(2)}) copy-start(s32[1024]{0:T(1024)S(1)} %fusion.89) | copy-start | bytes 12292
  56.0 203.5 %copy-start.21 = (f32[768]{0:T(1024)}, f32[768]{0:T(1024)S(1)}, u32[]{:S(2)}) copy-start(f32[768]{0:T(1024)S(1)} %convert_element_type.111) | copy-start | bytes 9220
  262.4 105.5 %all-gather.21.cloned.1.call-start = ((), (), s32[]{:S(2)}) async-start(), calls=%async_computation.14 | async-start | bytes 1327104 | tf_op jit(solution)/shard_map/all_gather | solution.py:130
  263.1 151.4 %all-gather.23.cloned.1.call-start = ((), (), s32[]{:S(2)}) async-start(), calls=%async_computation.16 | async-start | bytes 7864320 | tf_op jit(solution)/shard_map/all_gather | solution.py:176
  265.6 295.1 %reduce-scatter.11.cloned.1.call-start = ((), (), s32[]{:S(2)}) async-start(), calls=%async_computation.17 | async-start | bytes 15728640 | tf_op jit(solution)/shard_map/reduce_scatter | solution.py:181
  461.5 200.7 %reduce-scatter.9.cloned.1.call-start = ((), (), s32[]{:S(2)}) async-start(), calls=%async_computation.15 | async-start | bytes 15728640 | tf_op jit(solution)/shard_map/reduce_scatter | solution.py:155
  484.6 430.2 %reduce-scatter.21.cloned.1.call-start = ((), (), s32[]{:S(2)}) async-start(), calls=%async_computation.22 | async-start | bytes 2654208 | tf_op jit(solution)/shard_map/reduce_scatter | solution.py:208
  495.1 419.7 %reduce-scatter.23.cloned.1.call-start = ((), (), s32[]{:S(2)}) async-start(), calls=%async_computation.23 | async-start | bytes 2654208 | tf_op jit(solution)/shard_map/reduce_scatter | solution.py:209
  505.3 157.0 %copy-start.28 = (f32[1024]{0:T(1024)S(1)}, f32[1024]{0:T(1024)}, u32[]{:S(2)}) copy-start(f32[1024]{0:T(1024)} %copy-done.27) | copy-start | bytes 12292
  505.3 433.4 %reduce-scatter.13.cloned.1.call-start = ((), (), s32[]{:S(2)}) async-start(), calls=%async_computation.18 | async-start | bytes 2433024 | tf_op jit(solution)/shard_map/reduce_scatter | solution.py:212
  676.3 160.4 %copy-start.3 = (bf16[1,1024,768]{1,2,0:T(8,128)(2,1)S(1)}, bf16[1,1024,768]{1,2,0:T(8,128)(2,1)}, u32[]{:S(2)}) copy-start(bf16[1,1024,768]{1,2,0:T(8,128)(2,1)} %copy-done.2) | copy-start | bytes 4718596
  676.3 160.4 %copy-start.26 = (f32[1024]{0:T(1024)S(1)}, f32[1024]{0:T(1024)}, u32[]{:S(2)}) copy-start(f32[1024]{0:T(1024)} %copy-done.25) | copy-start | bytes 12292
  676.3 160.4 %copy-start.30 = (f32[768]{0:T(1024)S(1)}, f32[768]{0:T(1024)}, u32[]{:S(2)}) copy-start(f32[768]{0:T(1024)} %copy-done.29) | copy-start | bytes 9220
  676.3 160.4 %copy-start.32 = (f32[1024]{0:T(1024)S(1)}, f32[1024]{0:T(1024)}, u32[]{:S(2)}) copy-start(f32[1024]{0:T(1024)} %copy-done.31) | copy-start | bytes 12292
  839.6 203.7 %reduce-scatter.15.cloned.1.call-start = ((), (), s32[]{:S(2)}) async-start(), calls=%async_computation.19 | async-start | bytes 2433024 | tf_op jit(solution)/shard_map/reduce_scatter | solution.py:213
  844.0 303.0 %reduce-scatter.17.cloned.1.call-start = ((), (), s32[]{:S(2)}) async-start(), calls=%async_computation.20 | async-start | bytes 2433024 | tf_op jit(solution)/shard_map/reduce_scatter | solution.py:214
  848.6 403.1 %reduce-scatter.19.cloned.1.call-start = ((), (), s32[]{:S(2)}) async-start(), calls=%async_computation.21 | async-start | bytes 2433024 | tf_op jit(solution)/shard_map/reduce_scatter | solution.py:215
  (33 other events, 985.0 us)
Sparse Core Ops, SparseCore 0:
  10.9 56.7 all-gather.8
  70.7 52.9 all-gather.10
  126.6 52.9 all-gather.12
  182.3 52.9 all-gather.14
  237.4 39.9 all-gather.18
  279.4 45.1 all-gather.16
  326.7 41.0 all-gather.20
  369.4 45.1 all-gather.22
  461.6 99.0 reduce-scatter.10
  563.2 99.0 reduce-scatter.8
  666.3 68.9 reduce-scatter.20
  739.3 68.2 reduce-scatter.22
  839.7 98.9 reduce-scatter.12
  945.3 97.9 reduce-scatter.14
  1049.1 97.9 reduce-scatter.16
  1153.6 98.0 reduce-scatter.18
where the time goes:
time: 1270 us; the launch traced here: 1260 us
  waiting for transfers between devices  746 us (59%)
  matrix products  299 us (24%)
  blocking collectives  81.8 us (6%)
  local copies, waits for them, and re-layouts  57.7 us (5%)
  other arithmetic  57.1 us (4%)
  between operations  15.3 us (1%)
    dot_general x42, matrix products, dot_last(): lax.dot_general(left_side, right_side, (((1,), (1,)), ((), ())), preferre...  128 us
    reduce_scatter x1, waiting for transfers between devices, on_device(): lax.psum_scatter(grad_output_w, ('dp', 'tp'), scatter_dimension=0, tiled=...  105 us
    reduce_scatter x1, waiting for transfers between devices, on_device(): lax.psum_scatter(grad_key_w, ('dp', 'tp'), scatter_dimension=0, tiled=True)  105 us
    reduce_scatter x1, waiting for transfers between devices, on_device(): lax.psum_scatter(grad_value_w, ('dp', 'tp'), scatter_dimension=0, tiled=T...  104 us
    reduce_scatter x1, waiting for transfers between devices, on_device(): lax.psum_scatter(dot_plain(lax.slice_in_dim(active, 0, token_count * lax....  98.6 us
    dot_general x30, matrix products, dot_first(): lax.dot_general(left_side, right_side, (((0,), (0,)), ((), ())), preferre...  94.1 us
    unnamed x2, blocking collectives  81.8 us
    dot_general x30, matrix products, dot_plain(): return jnp.dot(left_side, right_side, preferred_element_type=jnp.float32)  76.9 us
  transfers between devices with their start and end apart: 16, of which 13 were waited for; matrix products, arithmetic and copies ran while one was open for 29% of the time, Pallas kernels for 0%

commit v1 on v0

--- a/solution.py
+++ b/solution.py
@@ -7,6 +7,28 @@
 HEADS = 12
 HEAD_DIM = 64
 SLOTS = 4
+
+
+def in_order(blocks, dim):
+    shape = list(blocks.shape[1:])
+    shape[dim] *= blocks.shape[0]
+    return jnp.moveaxis(blocks, 0, dim).reshape(shape)
+
+
+def ring_gather(x, axis, dim):
+    size = lax.axis_size(axis)
+    pairs = [(i, (i + 1) % size) for i in range(size)]
+    back = [(b, a) for a, b in pairs]
+    lower, upper = ([], [])
+    for lap in range(size - 1):
+        if lap % 2 == 0:
+            lower.append(lax.ppermute(lower[-1] if lower else x, axis, pairs))
+        else:
+            upper.append(lax.ppermute(upper[-1] if upper else x, axis, back))
+    parts = jnp.stack([*lower[::-1], x, *upper])
+    shift = lax.axis_index(axis) - len(lower)
+    parts = parts[(jnp.arange(size) - shift) % size]
+    return in_order(parts, dim)
 
 
 def segment_numbers(lengths, pack_len):
@@ -127,7 +149,7 @@
     )
     expand_full, reduce_full = (
         lax.all_gather(w_expand, "dp", axis=0, tiled=True),
-        lax.all_gather(w_reduce, "dp", axis=1, tiled=True),
+        ring_gather(w_reduce, "dp", 1),
     )
     gain_one = gain_one.astype(jnp.float32)
     gain_two = gain_two.astype(jnp.float32)

time: 1270 us -> 1230 us (0.969)
  waiting for transfers between devices: 746 us -> 688 us
  starting transfers between devices: 0.64 us -> 17.2 us
    all_gather x1 -> x0, waiting for transfers between devices: 33.1 us -> none  [on_device(): lax.all_gather(w_reduce, 'dp', axis=1, tiled=True)]
    all_gather x1, waiting for transfers between devices: 47.2 us -> 24.6 us  [on_device(): normed_rows = lax.all_gather(normed_feed, 'tp', axis=0, tiled=True)]
    ppermute x0 -> x7, waiting for transfers between devices: none -> 19.1 us  [the longest x4 18.3 us: ring_gather(): lower.append(lax.ppermute(lower[-1] if lower else x, axis, pairs))]
    ppermute x0 -> x7, starting transfers between devices: none -> 16.6 us  [the longest x3 13.2 us: ring_gather(): upper.append(lax.ppermute(upper[-1] if upper else x, axis, back))]
  transfers between devices with their start and end apart: 16 -> 22, of which waited for: 13 -> 16; matrix products, arithmetic and copies ran while one was open for 29% -> 30% of each run, Pallas kernels for 0% -> 0%
where the time goes in v1:
time: 1230 us; the launch traced here: 1220 us
  waiting for transfers between devices  688 us (56%)
  matrix products  299 us (24%)
  blocking collectives  81.9 us (7%)
  local copies, waits for them, and re-layouts  58.6 us (5%)
  other arithmetic  57.1 us (5%)
  starting transfers between devices  17.2 us (1%)
  between operations  15.4 us (1%)
    dot_general x42, matrix products, dot_last(): lax.dot_general(left_side, right_side, (((1,), (1,)), ((), ())), preferre...  128 us
    reduce_scatter x1, waiting for transfers between devices, on_device(): lax.psum_scatter(grad_key_w, ('dp', 'tp'), scatter_dimension=0, tiled=True)  105 us
    reduce_scatter x1, waiting for transfers between devices, on_device(): lax.psum_scatter(grad_output_w, ('dp', 'tp'), scatter_dimension=0, tiled=...  105 us
    reduce_scatter x1, waiting for transfers between devices, on_device(): lax.psum_scatter(grad_value_w, ('dp', 'tp'), scatter_dimension=0, tiled=T...  104 us
    reduce_scatter x1, waiting for transfers between devices, on_device(): lax.psum_scatter(dot_plain(lax.slice_in_dim(active, 0, token_count * lax....  98.8 us
    dot_general x30, matrix products, dot_first(): lax.dot_general(left_side, right_side, (((0,), (0,)), ((), ())), preferre...  94.2 us
    unnamed x2, blocking collectives  81.9 us
    dot_general x30, matrix products, dot_plain(): return jnp.dot(left_side, right_side, preferred_element_type=jnp.float32)  77.2 us
  transfers between devices with their start and end apart: 22, of which 16 were waited for; matrix products, arithmetic and copies ran while one was open for 30% of the time, Pallas kernels for 0%

profile of v1, /device:TPU:0, one launch (start us, length us, event | category | flops | bytes accessed | tf_op | source)
XLA Modules:
  0.0 1218.5 jit_solution(11331401852950997089)
XLA Ops:
  13.2 42.1 %all-reduce.5 = (bf16[768]{0:T(1024)(128)(2,1)S(1)}, bf16[768]{0:T(1024)(128)(2,1)S(1)}) all-reduce(bf16[768]{0:T(1024)(128)(2,1)S(1)} %dynamic-update-slice, bf16[768]{0:T(1024)(128)(2,1)S(1)} %dynamic-update-slice.1), channel_id=1, replica_groups=mesh['dp'=8,'tp'=4] {'dp','tp'}, use_global_device_ids=true, to_apply=%add | all-reduce | flops 1536 | bytes 6144
  56.0 11.7 all-gather.8.cloned.1.call-done
  73.3 50.4 %all-gather.10.cloned.1.call-done = bf16[768,768]{1,0:T(8,128)(2,1)} async-done(((bf16[24,768]{1,0:T(8,128)(2,1)}), bf16[768,768]{1,0:T(8,128)(2,1)}) %all-gather.10.cloned.1.call-update) | async-done | bytes 1179664 | tf_op jit(solution)/shard_map/all_gather | solution.py:144
  129.2 50.3 %all-gather.12.cloned.1.call-done = bf16[768,768]{1,0:T(8,128)(2,1)} async-done(((bf16[24,768]{1,0:T(8,128)(2,1)}), bf16[768,768]{1,0:T(8,128)(2,1)}) %all-gather.12.cloned.1.call-update) | async-done | bytes 1179664 | tf_op jit(solution)/shard_map/all_gather | solution.py:145
  185.3 68.7 %while.28 = (s32[]{:T(128)}, bf16[12,1024,64]{1,2,0:T(8,128)(2,1)S(1)}, f32[12,1024,1]{1,2,0:T(1,128)}, f32[12,1024,1]{1,2,0:T(1,128)}, s32[12,1024]{1,0:T(8,128...) while((s32[]{:T(128)}, ...), condition=%wide.region_7.8_spmd, body=%wide.region_4.7_spmd.sunk | while | flops 284227584 | bytes 13568109 | solution.py:165
  266.9 8.9 collective-permute-done
  301.7 24.6 %all-gather.16.cloned.1.call-done = bf16[4096,768]{0,1:T(8,128)(2,1)} async-done(((bf16[1024,768]{0,1:T(8,128)(2,1)}), bf16[4096,768]{0,1:T(8,128)(2,1)}) %all-gather.16.cloned.1.call-update) | async-done | bytes 6291472 | tf_op jit(solution)/shard_map/all_gather | solution.py:173
  326.3 10.5 fusion.106
  336.8 37.5 %all-gather.20.cloned.1.call-done = bf16[4096,768]{0,1:T(8,128)(2,1)} async-done(((bf16[1024,768]{0,1:T(8,128)(2,1)}), bf16[4096,768]{0,1:T(8,128)(2,1)}) %all-gather.20.cloned.1.call-update) | async-done | bytes 6291472 | tf_op jit(solution)/shard_map/all_gather | solution.py:198
  374.3 36.2 %add_convert_fusion = (bf16[4096,768]{1,0:T(8,128)(2,1)S(1)}, f32[4096,768]{1,0:T(8,128)}) fusion(f32[4096,768]{1,0:T(8,128)} %fusion.106, bf16[4096,768]{0,1:T(8,128)(2,1)} %all-gather.20.cloned.1.call-done, bf16[768,768]{0,1:T(8,128)(2,1)S(1)} %bitcast.256), kind=kOutput, calls=%fused_computation.65 | convolution fusion | flops 5058330624 | bytes 38928384 | tf_op jit(solution)/shard_map/dot_general | solution.py:73
  413.1 7.9 fusion.108
  421.1 11.1 multiply_convert_fusion.1
  436.0 7.9 fusion.107
  444.1 10.4 fusion.109
  454.5 10.1 fusion.112
  464.7 55.5 %reduce-scatter.11.cloned.1.call-done = f32[1024,768]{0,1:T(8,128)} async-done(((f32[4096,768]{0,1:T(8,128)}), f32[1024,768]{0,1:T(8,128)}) %reduce-scatter.11.cloned.1.call-update) | async-done | bytes 3145744 | tf_op jit(solution)/shard_map/reduce_scatter | solution.py:203
  523.2 98.8 %reduce-scatter.9.cloned.1.call-done = f32[1024,768]{0,1:T(8,128)} async-done(((f32[4096,768]{0,1:T(8,128)}), f32[1024,768]{0,1:T(8,128)}) %reduce-scatter.9.cloned.1.call-update) | async-done | bytes 3145744 | tf_op jit(solution)/shard_map/reduce_scatter | solution.py:177
  622.0 6.7 multiply_reduce_fusion.2
  636.0 160.3 %while.29 = (s32[]{:T(128)}, bf16[12,1024,64]{1,2,0:T(8,128)(2,1)S(1)}, bf16[12,1024,64]{1,2,0:T(8,128)(2,1)}, bf16[12,1024,64]{1,2,0:T(8,128)(2,1)}, s32[12,102...) while((s32[]{:T(128)}, ...), condition=%wide.region_16.17_spmd, body=%wide.region_14.16_spmd.sunk | while | flops 682949632 | bytes 33739908 | solution.py:212
  830.5 39.8 %all-reduce.4 = (f32[768]{0:T(1024)S(1)}, f32[768]{0:T(1024)S(1)}, f32[1]{0:T(128)}, f32[1]{0:T(128)}, f32[1]{0:T(128)}, /*index=5*/f32[]{:T(128)}) all-reduce(f32[768]{0:T(1024)S(1)} %get-tuple-element.155, f32[768]{0:T(1024)S(1)} %get-tuple-element.153, f32[1]{0:T(128)} %bitcast.72, ...), channel_id=8, replica_groups=mesh['dp'=8,'tp'=4] {'dp','tp'}, use_global_device_ids=true, to_apply=%region_24.25.clone | all-reduce | flops 1540 | bytes 12320
  874.7 23.9 %reduce-scatter.13.cloned.1.call-done = f32[24,768]{1,0:T(8,128)} async-done(((f32[768,768]{1,0:T(8,128)}), f32[24,768]{1,0:T(8,128)}) %reduce-scatter.13.cloned.1.call-update) | async-done | bytes 73744 | tf_op jit(solution)/shard_map/reduce_scatter | solution.py:234
  898.6 104.8 %reduce-scatter.15.cloned.1.call-done = f32[24,768]{1,0:T(8,128)} async-done(((f32[768,768]{1,0:T(8,128)}), f32[24,768]{1,0:T(8,128)}) %reduce-scatter.15.cloned.1.call-update) | async-done | bytes 73744 | tf_op jit(solution)/shard_map/reduce_scatter | solution.py:235
  1003.4 103.8 %reduce-scatter.17.cloned.1.call-done = f32[24,768]{1,0:T(8,128)} async-done(((f32[768,768]{1,0:T(8,128)}), f32[24,768]{1,0:T(8,128)}) %reduce-scatter.17.cloned.1.call-update) | async-done | bytes 73744 | tf_op jit(solution)/shard_map/reduce_scatter | solution.py:236
  1107.2 104.6 %reduce-scatter.19.cloned.1.call-done = f32[24,768]{1,0:T(8,128)} async-done(((f32[768,768]{1,0:T(8,128)}), f32[24,768]{1,0:T(8,128)}) %reduce-scatter.19.cloned.1.call-update) | async-done | bytes 73744 | tf_op jit(solution)/shard_map/reduce_scatter | solution.py:237
  (350 shorter events, 344.9 us)
Async XLA Ops:
  7.2 60.6 %all-gather.8.cloned.1.call-start = ((), (), s32[]{:S(2)}) async-start(), calls=%async_computation.8 | async-start | bytes 1216512 | tf_op jit(solution)/shard_map/all_gather | solution.py:143
  7.9 115.7 %all-gather.10.cloned.1.call-start = ((), (), s32[]{:S(2)}) async-start(), calls=%async_computation.9 | async-start | bytes 1216512 | tf_op jit(solution)/shard_map/all_gather | solution.py:144
  8.7 170.9 %all-gather.12.cloned.1.call-start = ((), (), s32[]{:S(2)}) async-start(), calls=%async_computation.10 | async-start | bytes 1216512 | tf_op jit(solution)/shard_map/all_gather | solution.py:145
  9.4 244.7 %all-gather.14.cloned.1.call-start = ((), (), s32[]{:S(2)}) async-start(), calls=%async_computation.11 | async-start | bytes 1216512 | tf_op jit(solution)/shard_map/all_gather | solution.py:146
  10.0 291.7 %all-gather.18.cloned.1.call-start = ((), (), s32[]{:S(2)}) async-start(), calls=%async_computation.13 | async-start | bytes 1327104 | tf_op jit(solution)/shard_map/all_gather | solution.py:151
  10.6 315.7 %all-gather.16.cloned.1.call-start = ((), (), s32[]{:S(2)}) async-start(), calls=%async_computation.12 | async-start | bytes 7864320 | tf_op jit(solution)/shard_map/all_gather | solution.py:173
  12.4 241.8 %copy-start.2 = (bf16[1,1024,768]{1,2,0:T(8,128)(2,1)}, bf16[1,1024,768]{1,2,0:T(8,128)(2,1)S(1)}, u32[]{:S(2)}) copy-start(bf16[1,1024,768]{1,2,0:T(8,128)(2,1)S(1)} %copy.42) | copy-start | bytes 4718596
  12.7 250.7 %copy-start.20 = (s32[1024]{0:T(1024)}, s32[1024]{0:T(1024)S(1)}, u32[]{:S(2)}) copy-start(s32[1024]{0:T(1024)S(1)} %fusion.89) | copy-start | bytes 12292
  262.4 111.9 %all-gather.20.cloned.1.call-start = ((), (), s32[]{:S(2)}) async-start(), calls=%async_computation.15 | async-start | bytes 7864320 | tf_op jit(solution)/shard_map/all_gather | solution.py:198
  265.1 255.2 %reduce-scatter.11.cloned.1.call-start = ((), (), s32[]{:S(2)}) async-start(), calls=%async_computation.16 | async-start | bytes 15728640 | tf_op jit(solution)/shard_map/reduce_scatter | solution.py:203
  265.1 10.6 collective-permute-start
  275.8 8.5 collective-permute-start.1
  275.8 9.2 collective-permute-start.4
  284.3 7.9 collective-permute-start.2
  284.9 8.4 collective-permute-start.5
  292.2 7.9 collective-permute-start.3
  293.3 7.7 collective-permute-start.6
  421.1 200.9 %reduce-scatter.9.cloned.1.call-start = ((), (), s32[]{:S(2)}) async-start(), calls=%async_computation.14 | async-start | bytes 15728640 | tf_op jit(solution)/shard_map/reduce_scatter | solution.py:177
  444.0 430.7 %reduce-scatter.21.cloned.1.call-start = ((), (), s32[]{:S(2)}) async-start(), calls=%async_computation.21 | async-start | bytes 2654208 | tf_op jit(solution)/shard_map/reduce_scatter | solution.py:230
  454.5 420.2 %reduce-scatter.23.cloned.1.call-start = ((), (), s32[]{:S(2)}) async-start(), calls=%async_computation.22 | async-start | bytes 2654208 | tf_op jit(solution)/shard_map/reduce_scatter | solution.py:231
  464.7 433.9 %reduce-scatter.13.cloned.1.call-start = ((), (), s32[]{:S(2)}) async-start(), calls=%async_computation.17 | async-start | bytes 2433024 | tf_op jit(solution)/shard_map/reduce_scatter | solution.py:234
  799.2 204.2 %reduce-scatter.15.cloned.1.call-start = ((), (), s32[]{:S(2)}) async-start(), calls=%async_computation.18 | async-start | bytes 2433024 | tf_op jit(solution)/shard_map/reduce_scatter | solution.py:235
  803.6 303.6 %reduce-scatter.17.cloned.1.call-start = ((), (), s32[]{:S(2)}) async-start(), calls=%async_computation.19 | async-start | bytes 2433024 | tf_op jit(solution)/shard_map/reduce_scatter | solution.py:236
  808.2 403.5 %reduce-scatter.19.cloned.1.call-start = ((), (), s32[]{:S(2)}) async-start(), calls=%async_computation.20 | async-start | bytes 2433024 | tf_op jit(solution)/shard_map/reduce_scatter | solution.py:237
  (39 other events, 1791.0 us)
Sparse Core Ops, SparseCore 0:
  10.9 56.7 all-gather.7
  70.7 52.9 all-gather.9
  126.6 52.9 all-gather.11
  182.3 52.9 all-gather.13
  237.3 40.5 all-gather.17
  279.9 46.3 all-gather.15
  327.9 46.3 all-gather.19
  421.2 99.0 reduce-scatter.10
  522.9 99.0 reduce-scatter.8
  625.9 68.9 reduce-scatter.20
  699.0 68.0 reduce-scatter.22
  799.3 99.2 reduce-scatter.12
  905.3 98.0 reduce-scatter.14
  1009.1 97.9 reduce-scatter.16
  1113.7 97.9 reduce-scatter.18
